TPU v7x, 256 devices: a whole 4x4x8 slice. The times are simulated.
256 devices in a mesh: lat: 8 (over x_hi, y), lon: 32 (over x_lo, z, core).
Axes of the slice: x: 4 (x_hi: 2, x_lo: 2; x = x_hi * 2 + x_lo), y: 4, z: 8, core: 2. Of those that a mesh axis runs over, the one named last changes fastest.
Arguments:
- tracer: float32 [100, 64, 4096], P(None, 'lat', 'lon'), may hold values from -100 to 100
- cotangent: float32 [100, 64, 4096], P(None, 'lat', 'lon'), may hold values from -6 to 6
- land_mask: int32 [64, 4096], P('lat', 'lon'), may hold values 0 or 1
- bottom: int32 [64, 4096], P('lat', 'lon'), may hold values from 25 to 100
- kappa: float32 [100], replicated, may hold values from 0.05 to 8
- w_in: bfloat16 [100, 512], replicated, may hold values from -0.625 to 0.625
- b_in: float32 [512], replicated, may hold values from -4 to 4
- w_out: bfloat16 [512, 100], replicated, may hold values from -0.25 to 0.25
- b_out: float32 [100], replicated, may hold values from 6 to 24
Outputs:
- tracer_adjoint: float32 [100, 64, 4096], P(None, 'lat', 'lon')
- grad_w_in: float32 [100, 512], replicated
- grad_b_in: float32 [512], replicated
- grad_w_out: float32 [512, 100], replicated
- grad_b_out: float32 [100], replicated
All inputs are finite; a program needn't handle non-finite values. No bound on the sum of `land_mask` on one device may be relied on, other than what follows from the above.
Results may differ from a plain program's by a relative error of at most 0.0069.
Values sent between devices are 32-bit elements; how exact they have to be, the bound alone decides.
A program may use at most 64 MiB of HBM per device.

v0:
```python
import math
import jax
import jax.numpy as jnp
from jax import lax
from jax.sharding import PartitionSpec as P

spread_coef = 0.15
level_eps = 1e-05


def with_halo(block, sides, width):
    for axis, dim in sides:
        count = lax.axis_size(axis)
        forward = [(i, i + 1) for i in range(count - 1)]
        forward.append((count - 1, 0))
        backward = [(target, source) for source, target in forward]
        low = lax.ppermute(
            lax.slice_in_dim(block, block.shape[dim] - width, None, axis=dim), axis, forward
        )
        high = lax.ppermute(lax.slice_in_dim(block, 0, width, axis=dim), axis, backward)
        block = jnp.concatenate([low, block, high], axis=dim)
    return block


def spread_local(field_pad, wet_pad):
    center = field_pad[:, 1:-1, 1:-1]
    wet_cells = wet_pad[:, 1:-1, 1:-1]
    neighbours = (
        (field_pad[:, 2:, 1:-1], wet_pad[:, 2:, 1:-1]),
        (field_pad[:, :-2, 1:-1], wet_pad[:, :-2, 1:-1]),
        (field_pad[:, 1:-1, :-2], wet_pad[:, 1:-1, :-2]),
        (field_pad[:, 1:-1, 2:], wet_pad[:, 1:-1, 2:]),
    )
    flux_total = jnp.zeros_like(center)
    for near_field, near_wet in neighbours:
        flux_total = flux_total + wet_cells * near_wet * (near_field - center)
    return center + spread_coef * flux_total


def column_solve(below, diagonal, above, right_side):

    def sweep_down(state_pair, row_items):
        ratio_prev, value_prev = state_pair
        below_row, diag_row, above_row, right_row = row_items
        pivot = diag_row - below_row * ratio_prev
        ratio_next = above_row / pivot
        value_next = (right_row - below_row * value_prev) / pivot
        return ((ratio_next, value_next), (ratio_next, value_next))

    zeros_row = jnp.zeros_like(right_side[0])
    _, (ratios, values) = lax.scan(
        sweep_down, (zeros_row, zeros_row), (below, diagonal, above, right_side), unroll=True
    )

    def sweep_up(later, row_items):
        ratio_row, value_row = row_items
        result_row = value_row - ratio_row * later
        return (result_row, result_row)

    _, solved = lax.scan(sweep_up, zeros_row, (ratios, values), reverse=True, unroll=True)
    return solved


def network(wet_tracer, radius, w_in, b_in, w_out, b_out):
    inputs = (wet_tracer / radius[:, None]).astype(jnp.bfloat16)
    pre_act = (
        lax.dot_general(w_in, inputs, (((0,), (0,)), ((), ())), preferred_element_type=jnp.float32)
        + b_in[:, None]
    )
    hidden = jax.nn.silu(pre_act).astype(jnp.bfloat16)
    logits = (
        lax.dot_general(w_out, hidden, (((0,), (0,)), ((), ())), preferred_element_type=jnp.float32)
        + b_out[:, None]
    )
    sinking = jax.nn.softplus(logits)
    return (inputs, pre_act, hidden, logits, sinking)


def coefficients(wet_cells, kappa_col, sinking):
    open_face = wet_cells * jnp.concatenate([wet_cells[1:], jnp.zeros_like(wet_cells[:1])], 0)
    down_coef = open_face * (kappa_col + sinking)
    up_coef = open_face * kappa_col
    prev_down = jnp.concatenate([jnp.zeros_like(down_coef[:1]), down_coef[:-1]], 0)
    prev_up = jnp.concatenate([jnp.zeros_like(up_coef[:1]), up_coef[:-1]], 0)
    diagonal = 1.0 + down_coef + prev_up
    return (open_face, down_coef, up_coef, prev_down, prev_up, diagonal)


def shards(tracer, cotangent, land_mask, bottom, kappa, w_in, b_in, w_out, b_out):
    level_count, lat_rows, lon_cols = tracer.shape
    column_count = lat_rows * lax.axis_size("lat") * lon_cols * lax.axis_size("lon")
    column_depth = (land_mask * bottom).astype(jnp.float32)
    stacked = jnp.concatenate([tracer, column_depth[None]], 0)
    padded = with_halo(stacked, (("lat", 1), ("lon", 2)), 1)
    lat_place = lax.axis_index("lat")
    upper_edge = jnp.where(lat_place == 0, 0.0, 1.0).astype(jnp.float32)
    lower_edge = jnp.where(lat_place == lax.axis_size("lat") - 1, 0.0, 1.0).astype(jnp.float32)
    lat_edge = jnp.concatenate(
        [upper_edge[None], jnp.ones((lat_rows,), jnp.float32), lower_edge[None]]
    )
    depth_pad = padded[-1] * lat_edge[:, None]
    level_ids = jnp.arange(level_count, dtype=jnp.float32)[:, None, None]
    wet_pad = (level_ids < depth_pad[None]).astype(jnp.float32)
    wet_cells = wet_pad[:, 1:-1, 1:-1]
    tracer_pad = padded[:level_count]
    mixed = spread_local(tracer_pad, wet_pad)
    wet_tracer = (wet_cells * tracer).reshape(level_count, -1)
    energy = lax.psum(jnp.sum(wet_tracer * wet_tracer, axis=1), ("lat", "lon"))
    radius = jnp.sqrt(energy / column_count + level_eps)
    inputs, pre_act, hidden, logits, sinking_flat = network(
        wet_tracer, radius, w_in, b_in, w_out, b_out
    )
    sinking = sinking_flat.reshape(tracer.shape)
    kappa_col = kappa[:, None, None]
    open_face, down_coef, up_coef, prev_down, prev_up, diagonal = coefficients(
        wet_cells, kappa_col, sinking
    )
    new_tracer = column_solve(-prev_down, diagonal, -up_coef, mixed)
    adjoint = column_solve(-prev_up, diagonal, -down_coef, cotangent)
    adjoint_pad = with_halo(adjoint, (("lat", 1), ("lon", 2)), 1)
    spread_back = spread_local(adjoint_pad, wet_pad)
    adjoint_next = jnp.concatenate([adjoint[1:], jnp.zeros_like(adjoint[:1])], 0)
    d_sinking = open_face * new_tracer * (adjoint_next - adjoint)
    d_logits = (d_sinking.reshape(level_count, -1) * jax.nn.sigmoid(logits)).astype(jnp.bfloat16)
    grad_out_t = lax.dot_general(
        d_logits, hidden, (((1,), (1,)), ((), ())), preferred_element_type=jnp.float32
    )
    grad_bout = jnp.sum(d_logits.astype(jnp.float32), axis=1)
    d_hidden = jnp.dot(w_out, d_logits, preferred_element_type=jnp.float32)
    gate_sig = jax.nn.sigmoid(pre_act)
    d_pre = (d_hidden * gate_sig * (1.0 + pre_act * (1.0 - gate_sig))).astype(jnp.bfloat16)
    grad_in = lax.dot_general(
        inputs, d_pre, (((1,), (1,)), ((), ())), preferred_element_type=jnp.float32
    )
    grad_bin = jnp.sum(d_pre.astype(jnp.float32), axis=1)[None]
    d_inputs = jnp.dot(w_in, d_pre, preferred_element_type=jnp.float32)
    level_part = jnp.sum(d_inputs * wet_tracer, axis=1)
    sum_in, sum_out_t, sum_bin, sum_bout, level_sum = lax.psum(
        (grad_in, grad_out_t, grad_bin, grad_bout, level_part), ("lat", "lon")
    )
    column_scale = 1.0 / math.sqrt(column_count)
    d_wet = (
        d_inputs / radius[:, None] - wet_tracer * (level_sum / (column_count * radius**3))[:, None]
    )
    tracer_adjoint = spread_back + wet_cells * d_wet.reshape(tracer.shape)
    grad_w_in = sum_in * column_scale
    grad_b_in = sum_bin[0] * column_scale
    grad_w_out = sum_out_t.T * column_scale
    grad_b_out = sum_bout * column_scale
    return (tracer_adjoint, grad_w_in, grad_b_in, grad_w_out, grad_b_out)


def solution(mesh):
    placed = (
        P(None, "lat", "lon"),
        P(None, "lat", "lon"),
        P("lat", "lon"),
        P("lat", "lon"),
        P(),
        P(),
        P(),
        P(),
        P(),
    )
    return jax.shard_map(
        shards,
        mesh=mesh,
        in_specs=placed,
        out_specs=(P(None, "lat", "lon"), P(), P(), P(), P()),
        check_vma=False,
    )
```

profile of v0, /device:TPU:2, one launch (start us, length us, event | category | flops | bytes accessed | tf_op | source)
XLA Modules:
  0.0 479.5 jit_solution(435788746220451003)
XLA Ops:
  7.2 0.7 convert_bitcast_fusion
  7.9 1.2 pad_maximum_fusion.23
  9.1 1.7 collective-permute-start
  10.8 4.1 collective-permute-start.1
  14.9 2.1 collective-permute-done
  16.9 1.2 pad_maximum_fusion
  19.2 4.3 collective-permute-start.3
  23.6 0.8 collective-permute-done.2
  25.4 0.9 copy-done.2
  26.7 0.7 copy-done.4
  27.5 2.3 fusion.735
  29.9 0.8 copy.1030
  30.7 81.1 %psum.42 = f32[100]{0:T(128)S(1)} all-reduce(f32[100]{0:T(128)S(1)} %get-tuple-element.618), channel_id=1, replica_groups=mesh['lat'=8,'lon'=32] {'lat','lon'}, use_global_device_ids=true, to_apply=%region_1.2 | all-reduce | flops 100 | bytes 800 | tf_op jit(solution)/shard_map/psum | solution.py:108
  111.8 1.9 fusion.5
  116.3 1.1 fusion.15
  125.0 1.0 fusion.834
  126.0 1.0 convert_reduce_fusion
  127.1 1.0 copy-done.10
  128.0 1.0 fusion.543
  129.1 2.5 multiply_reduce_fusion
  131.6 1.5 collective-permute-start.4
  133.7 76.5 %all-reduce.4 = (f32[100]{0:T(128)S(1)}, f32[1,512]{1,0:T(1,128)S(1)}, f32[100]{0:T(128)S(1)}) all-reduce(f32[100]{0:T(128)S(1)} %get-tuple-element.826, f32[1,512]{1,0:T(1,128)S(1)} %bitcast.5569, f32[100]{0:T(128)S(1)} %get-tuple-element.15), channel_id=1, replica_groups=mesh['lat'=8,'lon'=32] {'lat','lon'}, use_global_device_ids=true, to_apply=%region_3.4 | all-reduce | flops 712 | bytes 5696 | tf_op jit(solution)/shard_map/psum | solution.py:138
  210.3 1.1 multiply_subtract_fusion
  212.2 1.2 fusion.832
  213.3 1.5 copy.1024
  215.3 3.9 collective-permute-start.7
  219.6 0.9 copy.1033
  221.0 1.3 copy.1027
  222.3 3.0 fusion.9
  225.3 244.1 %all-reduce.8.cloned.1.call-done = (f32[100,512]{1,0:T(8,128)}, f32[100,512]{1,0:T(8,128)}) async-done(((f32[100,512]{1,0:T(8,128)}, f32[100,512]{1,0:T(8,128)}), (f32[100,512]{1,0:T(8,128)}, f32[100,512]{1,0:T(8,128)})) %all-reduce.8.cloned.1.call-update) | async-done | bytes 409616 | tf_op jit(solution)/shard_map/psum | solution.py:138
  469.3 1.6 broadcast_multiply_fusion.1
  471.0 1.6 multiply_bitcast_fusion
  (280 shorter events, 14.0 us)
Async XLA Ops:
  7.2 104.6 %copy-start = (bf16[100,512]{1,0:T(8,128)(2,1)S(1)}, bf16[100,512]{1,0:T(8,128)(2,1)}, u32[]{:S(2)}) copy-start(bf16[100,512]{1,0:T(8,128)(2,1)} %param.14) | copy-start | bytes 307204
  7.2 462.2 %all-reduce.8.cloned.1.call-start = ((), (), s32[]{:S(2)}) async-start(), calls=%async_computation | async-start | bytes 851968 | tf_op jit(solution)/shard_map/psum | solution.py:138
  9.1 7.8 %collective-permute-start = (f32[101,1,128]{2,1,0:T(1,128)S(1)}, f32[101,1,128]{2,1,0:T(1,128)S(1)}, u32[]{:S(2)}, u32[]{:S(2)}) collective-permute-start(f32[101,1,128]{2,1,0:T(1,128)S(1)} %get-tuple-element.624), channel_id=1, source_target_pairs={{0,32},{32,64},{64,96},{96,128},{128,160},{160,192},{192,224},{224... | collective-permute-start | bytes 155144 | tf_op jit(solution)/shard_map/ppermute | solution.py:17
  10.8 6.2 %collective-permute-start.1 = (f32[101,1,128]{2,1,0:T(1,128)S(1)}, f32[101,1,128]{2,1,0:T(1,128)S(1)}, u32[]{:S(2)}, u32[]{:S(2)}) collective-permute-start(f32[101,1,128]{2,1,0:T(1,128)S(1)} %get-tuple-element.625), channel_id=1, source_target_pairs={{32,0},{64,32},{96,64},{128,96},{160,128},{192,160},{224,192},{0,2... | collective-permute-start | bytes 155144 | tf_op jit(solution)/shard_map/ppermute | solution.py:20
  18.4 7.9 %copy-start.1 = (f32[100,8,128]{2,1,0:T(8,128)S(1)}, f32[100,8,128]{2,1,0:T(8,128)}, u32[]{:S(2)}) copy-start(f32[100,8,128]{2,1,0:T(8,128)} %param.9) | copy-start | bytes 1228804
  18.8 5.6 %collective-permute-start.2 = (f32[101,10,1]{0,1,2:T(8,128)S(1)}, f32[101,10,1]{0,1,2:T(8,128)S(1)}, u32[]{:S(2)}, u32[]{:S(2)}) collective-permute-start(f32[101,10,1]{0,1,2:T(8,128)S(1)} %copy.1020), channel_id=1, source_target_pairs={{0,1},{1,2},{2,3},{3,4},{4,5},{5,6},{6,7},{7,8},{8,9},{9,10},{10,1... | collective-permute-start | bytes 12128 | tf_op jit(solution)/shard_map/ppermute | solution.py:17
  19.2 5.6 %collective-permute-start.3 = (f32[101,10,1]{0,1,2:T(8,128)S(1)}, f32[101,10,1]{0,1,2:T(8,128)S(1)}, u32[]{:S(2)}, u32[]{:S(2)}) collective-permute-start(f32[101,10,1]{0,1,2:T(8,128)S(1)} %copy.1021), channel_id=1, source_target_pairs={{1,0},{2,1},{3,2},{4,3},{5,4},{6,5},{7,6},{8,7},{9,8},{10,9},{11,1... | collective-permute-start | bytes 12128 | tf_op jit(solution)/shard_map/ppermute | solution.py:20
  25.4 0.9 copy-start.2
  26.3 1.2 copy-start.11
  26.7 0.8 copy-start.4
  27.5 84.3 %copy-start.13 = (f32[512]{0:T(512)S(1)}, f32[512]{0:T(512)}, u32[]{:S(2)}) copy-start(f32[512]{0:T(512)} %param.15) | copy-start | bytes 6148
  111.8 1.9 copy-start.12
  111.8 1.9 copy-start.14
  113.7 1.0 copy-start.9
  113.7 1.1 copy-start.5
  115.2 1.1 copy-start.3
  119.0 2.4 copy-start.7
  126.0 2.0 copy-start.6
  127.0 1.0 copy-start.10
  131.6 80.4 %collective-permute-start.4 = (f32[100,1,128]{2,1,0:T(1,128)S(1)}, f32[100,1,128]{2,1,0:T(1,128)S(1)}, u32[]{:S(2)}, u32[]{:S(2)}) collective-permute-start(f32[100,1,128]{2,1,0:T(1,128)S(1)} %get-tuple-element.627), channel_id=1, source_target_pairs={{32,0},{64,32},{96,64},{128,96},{160,128},{192,160},{224,192},{0,2... | collective-permute-start | bytes 153608 | tf_op jit(solution)/shard_map/ppermute | solution.py:20
  133.1 78.9 %collective-permute-start.5 = (f32[100,1,128]{2,1,0:T(1,128)S(1)}, f32[100,1,128]{2,1,0:T(1,128)S(1)}, u32[]{:S(2)}, u32[]{:S(2)}) collective-permute-start(f32[100,1,128]{2,1,0:T(1,128)S(1)} %get-tuple-element.626), channel_id=1, source_target_pairs={{0,32},{32,64},{64,96},{96,128},{128,160},{160,192},{192,224},{224... | collective-permute-start | bytes 153608 | tf_op jit(solution)/shard_map/ppermute | solution.py:17
  214.8 5.7 %collective-permute-start.6 = (f32[100,10,1]{0,1,2:T(8,128)S(1)}, f32[100,10,1]{0,1,2:T(8,128)S(1)}, u32[]{:S(2)}, u32[]{:S(2)}) collective-permute-start(f32[100,10,1]{0,1,2:T(8,128)S(1)} %copy.1024), channel_id=1, source_target_pairs={{0,1},{1,2},{2,3},{3,4},{4,5},{5,6},{6,7},{7,8},{8,9},{9,10},{10,1... | collective-permute-start | bytes 12008 | tf_op jit(solution)/shard_map/ppermute | solution.py:17
  215.3 5.7 %collective-permute-start.7 = (f32[100,10,1]{0,1,2:T(8,128)S(1)}, f32[100,10,1]{0,1,2:T(8,128)S(1)}, u32[]{:S(2)}, u32[]{:S(2)}) collective-permute-start(f32[100,10,1]{0,1,2:T(8,128)S(1)} %copy.1026), channel_id=1, source_target_pairs={{1,0},{2,1},{3,2},{4,3},{5,4},{6,5},{7,6},{8,7},{9,8},{10,9},{11,1... | collective-permute-start | bytes 12008 | tf_op jit(solution)/shard_map/ppermute | solution.py:20
  220.5 1.8 copy-start.8
Sparse Core Ops, SparseCore 0:
  220.7 248.6 all-reduce.7
where the time goes:
time: 480 us; the launch traced here: 479 us
  waiting for transfers between devices  247 us (51%)
  blocking collectives  158 us (33%)
  other arithmetic  22.1 us (5%)
  starting transfers between devices  16.1 us (3%)
  between operations  15.9 us (3%)
  local copies, waits for them, and re-layouts  12.7 us (3%)
  matrix products  8.1 us (2%)
    psum x1, waiting for transfers between devices, shards(): lax.psum((grad_in, grad_out_t, grad_bin, grad_bout, level_part), ('lat',...  244 us
    psum x1, blocking collectives, shards(): energy = lax.psum(jnp.sum(wet_tracer * wet_tracer, axis=1), ('lat', 'lon'))  81.1 us
    psum x1, blocking collectives, shards(): lax.psum((grad_in, grad_out_t, grad_bin, grad_bout, level_part), ('lat',...  76.5 us
    ppermute x4, starting transfers between devices, with_halo(): lax.ppermute(lax.slice_in_dim(block, 0, width, axis=dim), axis, backward)  13.7 us
  transfers between devices with their start and end apart: 9, of which 3 were waited for; matrix products, arithmetic and copies ran while one was open for 2% of the time, Pallas kernels for 0%

commit v1 on v0

--- a/solution.py
+++ b/solution.py
@@ -105,7 +105,9 @@
     tracer_pad = padded[:level_count]
     mixed = spread_local(tracer_pad, wet_pad)
     wet_tracer = (wet_cells * tracer).reshape(level_count, -1)
-    energy = lax.psum(jnp.sum(wet_tracer * wet_tracer, axis=1), ("lat", "lon"))
+    own = jnp.sum(wet_tracer * wet_tracer, axis=1)
+    parts = lax.all_gather(own, ("lat", "lon"))
+    energy = jnp.sum(parts, axis=0)
     radius = jnp.sqrt(energy / column_count + level_eps)
     inputs, pre_act, hidden, logits, sinking_flat = network(
         wet_tracer, radius, w_in, b_in, w_out, b_out

time: 480 us -> 649 us (1.35)
  waiting for transfers between devices: 247 us -> 489 us
  blocking collectives: 158 us -> 75.9 us
    unnamed x1 -> x3, waiting for transfers between devices: 0.02 us -> 242 us
    psum x1 -> x0, blocking collectives: 81.1 us -> none  [shards(): energy = lax.psum(jnp.sum(wet_tracer * wet_tracer, axis=1), ('lat', 'lon'))]
  transfers between devices with their start and end apart: 9 -> 10, of which waited for: 3 -> 4; matrix products, arithmetic and copies ran while one was open for 2% -> 2% of each run, Pallas kernels for 0% -> 0%
where the time goes in v1:
time: 649 us
  waiting for transfers between devices  489 us (75%)
  blocking collectives  75.9 us (12%)
  other arithmetic  24.2 us (4%)
  local copies, waits for them, and re-layouts  18.8 us (3%)
  starting transfers between devices  17.7 us (3%)
  between operations  15.9 us (2%)
  matrix products  7.43 us (1%)
    psum x1, waiting for transfers between devices, shards(): lax.psum((grad_in, grad_out_t, grad_bin, grad_bout, level_part), ('lat',...  244 us
    unnamed x3, waiting for transfers between devices  242 us
    psum x1, blocking collectives, shards(): lax.psum((grad_in, grad_out_t, grad_bin, grad_bout, level_part), ('lat',...  75.9 us
    ppermute x4, starting transfers between devices, with_halo(): lax.ppermute(lax.slice_in_dim(block, 0, width, axis=dim), axis, backward)  15.7 us
  transfers between devices with their start and end apart: 10, of which 4 were waited for; matrix products, arithmetic and copies ran while one was open for 2% of the time, Pallas kernels for 0%

profile of v1, /device:TPU:2, one launch (start us, length us, event | category | flops | bytes accessed | tf_op | source)
XLA Modules:
  0.0 648.8 jit_solution(436478011480141905)
XLA Ops:
  7.9 1.2 pad_maximum_fusion.23
  9.1 1.7 collective-permute-start
  10.8 4.1 collective-permute-start.1
  14.9 2.1 collective-permute-done
  16.9 1.2 pad_maximum_fusion
  18.1 1.2 fusion.831
  19.3 1.5 copy.1020
  21.3 4.3 collective-permute-start.3
  27.8 0.9 copy-done.3
  29.4 2.3 fusion.735
  32.9 3.3 fusion.15
  37.1 242.1 %all-reduce.10.cloned.1.call-done = f32[25600]{0:T(1024)} async-done(((f32[25600]{0:T(1024)}), f32[25600]{0:T(1024)}) %all-reduce.10.cloned.1.call-update) | async-done | bytes 102416
  279.2 1.1 reshape.55
  280.5 1.9 fusion.5
  292.4 1.0 fusion.834
  293.4 1.1 convert_reduce_fusion
  294.5 1.0 copy-done.11
  295.5 1.0 fusion.543
  296.5 1.8 multiply_reduce_fusion
  298.3 3.5 collective-permute-start.4
  301.8 75.9 %all-reduce.5 = (f32[100]{0:T(128)S(1)}, f32[1,512]{1,0:T(1,128)S(1)}, f32[100]{0:T(128)S(1)}) all-reduce(f32[100]{0:T(128)S(1)} %get-tuple-element.826, f32[1,512]{1,0:T(1,128)S(1)} %bitcast.5569, f32[100]{0:T(128)S(1)} %get-tuple-element.15), channel_id=1, replica_groups=mesh['lat'=8,'lon'=32] {'lat','lon'}, use_global_device_ids=true, to_apply=%region_3.4 | all-reduce | flops 712 | bytes 5696 | tf_op jit(solution)/shard_map/psum | solution.py:140
  377.7 0.9 multiply_subtract_fusion
  379.4 1.4 fusion.832
  380.8 1.5 copy.1024
  382.3 1.5 copy.1026
  383.8 3.9 collective-permute-start.7
  388.2 1.9 copy.1033
  390.5 1.3 copy.1027
  391.8 3.1 fusion.9
  394.9 243.8 %all-reduce.12.cloned.1.call-done = (f32[100,512]{1,0:T(8,128)}, f32[100,512]{1,0:T(8,128)}) async-done(((f32[100,512]{1,0:T(8,128)}, f32[100,512]{1,0:T(8,128)}), (f32[100,512]{1,0:T(8,128)}, f32[100,512]{1,0:T(8,128)})) %all-reduce.12.cloned.1.call-update) | async-done | bytes 409616 | tf_op jit(solution)/shard_map/psum | solution.py:140
  638.7 1.6 broadcast_multiply_fusion.1
  640.4 1.6 multiply_bitcast_fusion
  (290 shorter events, 16.4 us)
Async XLA Ops:
  7.2 273.3 %copy-start = (bf16[100,512]{1,0:T(8,128)(2,1)S(1)}, bf16[100,512]{1,0:T(8,128)(2,1)}, u32[]{:S(2)}) copy-start(bf16[100,512]{1,0:T(8,128)(2,1)} %param.14) | copy-start | bytes 307204
  7.2 272.1 %all-reduce.10.cloned.1.call-start = ((), (), s32[]{:S(2)}) async-start(), calls=%async_computation | async-start | bytes 204800
  9.1 7.8 %collective-permute-start = (f32[101,1,128]{2,1,0:T(1,128)S(1)}, f32[101,1,128]{2,1,0:T(1,128)S(1)}, u32[]{:S(2)}, u32[]{:S(2)}) collective-permute-start(f32[101,1,128]{2,1,0:T(1,128)S(1)} %get-tuple-element.624), channel_id=1, source_target_pairs={{0,32},{32,64},{64,96},{96,128},{128,160},{160,192},{192,224},{224... | collective-permute-start | bytes 155144 | tf_op jit(solution)/shard_map/ppermute | solution.py:17
  10.8 6.2 collective-permute-start.1
  19.3 9.4 %copy-start.1 = (f32[100,8,128]{2,1,0:T(8,128)S(1)}, f32[100,8,128]{2,1,0:T(8,128)}, u32[]{:S(2)}) copy-start(f32[100,8,128]{2,1,0:T(8,128)} %param.9) | copy-start | bytes 1228804
  20.9 5.6 collective-permute-start.2
  21.3 5.6 collective-permute-start.3
  26.9 0.9 copy-start.2
  27.8 0.9 copy-start.3
  28.7 0.7 copy-start.13
  32.0 0.6 copy-start.12
  32.7 606.0 %all-reduce.12.cloned.1.call-start = ((), (), s32[]{:S(2)}) async-start(), calls=%async_computation.1 | async-start | bytes 851968 | tf_op jit(solution)/shard_map/psum | solution.py:140
  32.9 3.3 copy-start.9
  32.9 4.2 copy-start.10
  36.2 244.2 %copy-start.15 = (f32[512]{0:T(512)S(1)}, f32[512]{0:T(512)}, u32[]{:S(2)}) copy-start(f32[512]{0:T(512)} %param.15) | copy-start | bytes 6148
  280.5 1.9 copy-start.14
  280.5 1.9 copy-start.16
  283.4 1.0 copy-start.7
  286.0 2.4 copy-start.8
  291.4 0.8 copy-start.4
  293.4 2.1 copy-start.6
  294.5 1.0 copy-start.11
  296.5 82.7 %copy-start.5 = (f32[100,8,128]{2,1,0:T(8,128)S(1)}, f32[100,8,128]{2,1,0:T(8,128)}, u32[]{:S(2)}) copy-start(f32[100,8,128]{2,1,0:T(8,128)} %copy-done.4) | copy-start | bytes 1228804
  298.3 80.8 %collective-permute-start.4 = (f32[100,1,128]{2,1,0:T(1,128)S(1)}, f32[100,1,128]{2,1,0:T(1,128)S(1)}, u32[]{:S(2)}, u32[]{:S(2)}) collective-permute-start(f32[100,1,128]{2,1,0:T(1,128)S(1)} %get-tuple-element.627), channel_id=1, source_target_pairs={{32,0},{64,32},{96,64},{128,96},{160,128},{192,160},{224,192},{0,2... | collective-permute-start | bytes 153608 | tf_op jit(solution)/shard_map/ppermute | solution.py:20
  301.8 77.4 %collective-permute-start.5 = (f32[100,1,128]{2,1,0:T(1,128)S(1)}, f32[100,1,128]{2,1,0:T(1,128)S(1)}, u32[]{:S(2)}, u32[]{:S(2)}) collective-permute-start(f32[100,1,128]{2,1,0:T(1,128)S(1)} %get-tuple-element.626), channel_id=1, source_target_pairs={{0,32},{32,64},{64,96},{96,128},{128,160},{160,192},{192,224},{224... | collective-permute-start | bytes 153608 | tf_op jit(solution)/shard_map/ppermute | solution.py:17
  382.2 7.8 %collective-permute-start.6 = (f32[100,10,1]{0,1,2:T(8,128)S(1)}, f32[100,10,1]{0,1,2:T(8,128)S(1)}, u32[]{:S(2)}, u32[]{:S(2)}) collective-permute-start(f32[100,10,1]{0,1,2:T(8,128)S(1)} %copy.1024), channel_id=1, source_target_pairs={{0,1},{1,2},{2,3},{3,4},{4,5},{5,6},{6,7},{7,8},{8,9},{9,10},{10,1... | collective-permute-start | bytes 12008 | tf_op jit(solution)/shard_map/ppermute | solution.py:17
  383.8 6.7 %collective-permute-start.7 = (f32[100,10,1]{0,1,2:T(8,128)S(1)}, f32[100,10,1]{0,1,2:T(8,128)S(1)}, u32[]{:S(2)}, u32[]{:S(2)}) collective-permute-start(f32[100,10,1]{0,1,2:T(8,128)S(1)} %copy.1026), channel_id=1, source_target_pairs={{1,0},{2,1},{3,2},{4,3},{5,4},{6,5},{7,6},{8,7},{9,8},{10,9},{11,1... | collective-permute-start | bytes 12008 | tf_op jit(solution)/shard_map/ppermute | solution.py:20
Sparse Core Ops, SparseCore 0:
  32.8 246.3 all-reduce.9
  390.2 248.4 all-reduce.11
